TPU v7x, 32 devices: a whole 2x2x4 slice. The times are simulated.
32 devices in a mesh: ctx: 4 (over z), node: 4 (over y, core), local: 2 (over x).
Axes of the slice: x: 2, y: 2, z: 4, core: 2. Of those that a mesh axis runs over, the one named last changes fastest.
Arguments:
- tokens: bfloat16 [1024, 3584], P(('node', 'local'), 'ctx'), may hold values from -6 to 6
- expert_ids: int32 [1024, 4], P(('node', 'local')), may hold values from 0 to 7, as said below
- route_scores: float32 [1024, 4], P(('node', 'local')), may hold values from 0.05 to 1
- w_gate: bfloat16 [8, 3584, 2048], P(('node', 'local'), None, 'ctx'), may hold values from -0.09375 to 0.09375
- w_up: bfloat16 [8, 3584, 2048], P(('node', 'local'), None, 'ctx'), may hold values from -0.09375 to 0.09375
- w_down: bfloat16 [8, 2048, 3584], P(('node', 'local'), None, 'ctx'), may hold values from -0.125 to 0.125
- shared_gate: bfloat16 [3584, 2048], P(None, 'ctx'), may hold values from -0.09375 to 0.09375
- shared_up: bfloat16 [3584, 2048], P(None, 'ctx'), may hold values from -0.09375 to 0.09375
- shared_down: bfloat16 [2048, 3584], P(None, 'ctx'), may hold values from -0.125 to 0.125
Outputs:
- mixed: bfloat16 [1024, 3584], P(('node', 'local'), 'ctx')
Inputs may be any that keep to these rules, and one draw needn't show every extreme that they name: `expert_ids`: each row names 4 different experts: two in each of two different node groups, where expert e lies in group e // 2. In each aligned block of 128 rows (the rows of one index of node+local) no group is named by more than 80 rows and no expert more than 80 times; one group, the same in every block, is named by exactly 80 rows in every block, and one of its experts, the same in every block, exactly 80 times.
All inputs are finite; a program needn't handle non-finite values.
Results may differ from a plain program's by a relative error of at most 0.0064.
Values may be sent and summed in bfloat16 or wider, within the bound.
A program may use at most 64 MiB of HBM per device.

v0:
```python
import jax
import jax.numpy as jnp
from jax import lax
from jax.sharding import PartitionSpec as P

route_scale = 2.5


def matmul(left_side, right_side):
    return jnp.dot(left_side, right_side, preferred_element_type=jnp.float32)


def local(
    tokens, expert_ids, route_scores, w_gate, w_up, w_down, shared_gate, shared_up, shared_down
):
    tok_count = tokens.shape[0]
    feat_local = tokens.shape[1]
    top_count = expert_ids.shape[1]
    group_count = lax.axis_size("node")
    member_count = lax.axis_size("local")
    expert_count = group_count * member_count
    group_cap = (10 * tok_count + 4 * group_count - 1) // (4 * group_count)
    capacity = (2 * group_cap + member_count - 1) // member_count
    slot_total = expert_count * capacity
    gate_local = w_gate[0]
    up_local = w_up[0]
    down_local = w_down[0]
    out_width = down_local.shape[1]
    scaled = route_scale * route_scores / jnp.sum(route_scores, axis=1, keepdims=True)
    gate_weights = lax.optimization_barrier(scaled.astype(jnp.bfloat16)).astype(jnp.float32)
    group_range = jnp.arange(group_count, dtype=jnp.int32)
    group_onehot = (expert_ids // member_count)[:, :, None] == group_range[None, None, :]
    flat_ids = expert_ids.reshape(-1)
    pair_count = flat_ids.shape[0]
    onehot = (flat_ids[:, None] == jnp.arange(expert_count, dtype=jnp.int32)[None, :]).astype(
        jnp.int32
    )
    earlier = jnp.cumsum(onehot, axis=0) - onehot
    ranking = jnp.sum(earlier * onehot, axis=1)
    pair_slot = flat_ids * capacity + ranking
    pair_token = jnp.arange(pair_count, dtype=jnp.int32) // top_count
    matches = pair_slot[None, :] == jnp.arange(slot_total, dtype=jnp.int32)[:, None]
    slot_token = jnp.where(
        jnp.any(matches, axis=1),
        jnp.sum(jnp.where(matches, pair_token[None, :], 0), axis=1),
        tok_count,
    )
    padded_tokens = jnp.concatenate([tokens, jnp.zeros((1, feat_local), tokens.dtype)], axis=0)
    send_rows = padded_tokens[slot_token].reshape(group_count, member_count, capacity * feat_local)
    arrived = lax.all_to_all(
        lax.all_to_all(send_rows, "node", split_axis=0, concat_axis=0, tiled=True),
        "local",
        split_axis=1,
        concat_axis=1,
        tiled=True,
    )
    routed_rows = arrived.reshape(slot_total, feat_local)
    stacked = jnp.concatenate([routed_rows, tokens], axis=0)
    segment = lax.all_gather(stacked, "ctx", axis=1, tiled=True)
    routed_part = segment[:slot_total]
    shared_part = segment[slot_total:]
    gate_routed = matmul(routed_part, gate_local)
    up_routed = matmul(routed_part, up_local)
    gate_shared = matmul(shared_part, shared_gate)
    up_shared = matmul(shared_part, shared_up)
    routed_hidden = (jax.nn.silu(gate_routed) * up_routed).astype(jnp.bfloat16)
    shared_hidden = (jax.nn.silu(gate_shared) * up_shared).astype(jnp.bfloat16)
    hidden_stack = jnp.concatenate([routed_hidden, shared_hidden], axis=0)
    segment = lax.all_gather(hidden_stack, "ctx", axis=1, tiled=True)
    routed_out = matmul(segment[:slot_total], down_local)
    shared_out = matmul(segment[slot_total:], shared_down)
    routed_bf = routed_out.astype(jnp.bfloat16)
    sendback = routed_bf.reshape(group_count, member_count, capacity * out_width)
    returned = lax.all_to_all(
        lax.all_to_all(sendback, "node", split_axis=0, concat_axis=0, tiled=True),
        "local",
        split_axis=1,
        concat_axis=1,
        tiled=True,
    )
    returned = returned.reshape(slot_total, out_width)
    pair_out = returned[pair_slot].reshape(tok_count, top_count, out_width).astype(jnp.float32)
    weighted = gate_weights[:, :, None] * pair_out
    group_sum = jnp.einsum(
        "tkg,tkd->tgd", group_onehot.astype(jnp.float32), weighted, precision=lax.Precision.HIGHEST
    )
    rounded = lax.optimization_barrier(group_sum.astype(jnp.bfloat16)).astype(jnp.float32)
    routed_sum = jnp.sum(rounded, axis=1)
    mixed = shared_out + routed_sum
    return mixed.astype(jnp.bfloat16)


def solution(mesh):
    return jax.shard_map(
        local,
        mesh=mesh,
        in_specs=(
            P(("node", "local"), "ctx"),
            P(("node", "local"), None),
            P(("node", "local"), None),
            P(("node", "local"), None, "ctx"),
            P(("node", "local"), None, "ctx"),
            P(("node", "local"), None, "ctx"),
            P(None, "ctx"),
            P(None, "ctx"),
            P(None, "ctx"),
        ),
        out_specs=P(("node", "local"), "ctx"),
        check_vma=False,
    )
```

profile of v0, /device:TPU:0, one launch (start us, length us, event | category | flops | bytes accessed | tf_op | source)
XLA Modules:
  0.0 292.3 jit_solution(5308196414685565889)
XLA Ops:
  6.5 0.8 copy.43
  7.3 0.1 eq.52
  7.4 0.1 reshape.109
  7.6 1.1 reduce-window.6
  8.7 0.2 slice_reduce_fusion
  9.0 0.1 fusion.39
  9.1 0.2 fusion.29
  9.3 0.2 select_reduce_fusion
  9.5 1.0 concatenate.9
  10.5 3.1 %gather_fusion = bf16[640,896]{1,0:T(8,128)(2,1)S(1)} fusion(bf16[129,896]{1,0:T(8,128)(2,1)S(1)} %concatenate.9, s32[1024]{0:T(1024)S(1)} %pad_clamp_fusion.1), kind=kCustom, calls=%fused_computation | custom fusion | bytes 2296320 | tf_op jit(solution)/shard_map/gather | solution.py:49
  13.6 0.4 reshape.111
  14.0 19.6 %all_to_all.20 = bf16[4,2,71680]{2,1,0:T(2,128)(2,1)S(1)} all-to-all(bf16[4,2,71680]{2,1,0:T(2,128)(2,1)S(1)} %reshape.111), channel_id=1, replica_groups=mesh['ctx'=4,'node'=4,'local'=2] {'node'}, dimensions={0} | all-to-all | bytes 2293760 | tf_op jit(solution)/shard_map/all_to_all | solution.py:51
  33.5 0.6 copy.45
  34.1 17.1 %all_to_all.21 = bf16[4,2,71680]{2,0,1:T(4,128)(2,1)S(1)} all-to-all(bf16[4,2,71680]{2,0,1:T(4,128)(2,1)S(1)} %copy.45), channel_id=1, replica_groups=mesh['ctx'=4,'node'=4,'local'=2] {'local'}, dimensions={1} | all-to-all | bytes 2293760 | tf_op jit(solution)/shard_map/all_to_all | solution.py:50
  51.3 1.2 copy.46
  52.4 0.8 reshape.112
  53.3 1.2 pad_maximum_fusion
  54.5 0.0 all-gather.3.cloned.1.call-update
  54.5 0.0 all-gather.5.cloned.1.call-start
  54.6 102.0 %all-gather.3.cloned.1.call-done = bf16[768,3584]{1,0:T(8,128)(2,1)} async-done(((bf16[768,896]{1,0:T(8,128)(2,1)}), bf16[768,3584]{1,0:T(8,128)(2,1)}) %all-gather.3.cloned.1.call-update) | async-done | bytes 5505040 | tf_op jit(solution)/shard_map/all_gather | solution.py:59
  156.6 6.1 %fusion.2 = f32[640,512]{1,0:T(8,128)S(1)} fusion(bf16[768,3584]{1,0:T(8,128)(2,1)} %all-gather.3.cloned.1.call-done, bf16[1,3584,512]{2,1,0:T(8,128)(2,1)} %param.12), kind=kOutput, calls=%fused_computation.4 | convolution fusion | flops 2348810240 | bytes 9568256 | tf_op jit(solution)/shard_map/dot_general | solution.py:10
  162.7 0.0 copy-done
  162.7 0.0 copy-start.6
  162.7 0.6 fusion.34
  163.3 1.4 copy-done.6
  164.7 2.6 fusion.24
  167.4 0.6 fusion.31
  168.0 0.9 pad_maximum_fusion.1
  169.0 0.0 all-gather.5.cloned.1.call-update
  169.0 61.9 %all-gather.5.cloned.1.call-done = bf16[768,2048]{1,0:T(8,128)(2,1)} async-done(((bf16[768,512]{1,0:T(8,128)(2,1)}), bf16[768,2048]{1,0:T(8,128)(2,1)}) %all-gather.5.cloned.1.call-update) | async-done | bytes 3145744 | tf_op jit(solution)/shard_map/all_gather | solution.py:69
  230.9 5.7 %fusion.11 = bf16[640,896]{1,0:T(8,128)(2,1)S(1)} fusion(bf16[1,2048,896]{2,1,0:T(8,128)(2,1)} %param.14, bf16[768,2048]{1,0:T(8,128)(2,1)} %all-gather.5.cloned.1.call-done), kind=kOutput, calls=%fused_computation.14 | convolution fusion | flops 2349383680 | bytes 7438336 | tf_op jit(solution)/shard_map/dot_general | solution.py:10
  236.6 0.4 reshape.113
  237.0 18.0 %all_to_all.22 = bf16[4,2,71680]{2,1,0:T(2,128)(2,1)S(1)} all-to-all(bf16[4,2,71680]{2,1,0:T(2,128)(2,1)S(1)} %reshape.113), channel_id=1, replica_groups=mesh['ctx'=4,'node'=4,'local'=2] {'node'}, dimensions={0} | all-to-all | bytes 2293760 | tf_op jit(solution)/shard_map/all_to_all | solution.py:75
  255.0 1.6 copy.49
  256.6 3.8 %all-to-all-start.3 = ((bf16[4,2,71680]{2,0,1:T(4,128)(2,1)}), bf16[4,2,71680]{2,0,1:T(4,128)(2,1)S(1)}, u32[]{:S(2)}, u32[]{:S(2)}) async-start(bf16[4,2,71680]{2,0,1:T(4,128)(2,1)} %copy.49), calls=%async_computation.3 | async-start | bytes 2293760 | tf_op jit(solution)/shard_map/all_to_all | solution.py:74
  260.4 0.1 copy.51
  260.5 0.1 mul.67
  260.6 0.1 copy.47
  260.8 0.1 copy.48
  260.9 13.9 %all-to-all-done.3 = bf16[4,2,71680]{2,0,1:T(4,128)(2,1)S(1)} async-done(((bf16[4,2,71680]{2,0,1:T(4,128)(2,1)}), bf16[4,2,71680]{2,0,1:T(4,128)(2,1)S(1)}, u32[]{:S(2)}, u32[]{:S(2)}) %all-to-all-start.3) | async-done | bytes 1146912 | tf_op jit(solution)/shard_map/all_to_all | solution.py:74
  274.9 1.2 copy.50
  276.0 0.8 reshape.114
  276.9 2.1 gather_fusion.1
  278.9 0.5 reshape.115
  279.4 0.0 copy-start.1
  279.4 2.3 fusion.16
  281.7 1.3 convert_reduce_fusion
  283.0 2.5 fusion.30
  (25 shorter events, 0.2 us)
Async XLA Ops:
  6.5 150.0 %all-gather.3.cloned.1.call-start = ((), (), s32[]{:S(2)}) async-start(), calls=%async_computation.4 | async-start | bytes 6881280 | tf_op jit(solution)/shard_map/all_gather | solution.py:59
  51.3 2.0 copy-start.2
  54.5 176.4 %all-gather.5.cloned.1.call-start = ((), (), s32[]{:S(2)}) async-start(), calls=%async_computation.5 | async-start | bytes 3932160 | tf_op jit(solution)/shard_map/all_gather | solution.py:69
  156.6 6.1 %copy-start = (bf16[3584,512]{1,0:T(8,128)(2,1)S(1)}, bf16[3584,512]{1,0:T(8,128)(2,1)}, u32[]{:S(2)}) copy-start(bf16[3584,512]{1,0:T(8,128)(2,1)} %param.15) | copy-start | bytes 11010052
  156.6 6.1 %copy-start.3 = (bf16[768,3584]{1,0:T(8,128)(2,1)S(1)}, bf16[768,3584]{1,0:T(8,128)(2,1)}, u32[]{:S(2)}) copy-start(bf16[768,3584]{1,0:T(8,128)(2,1)} %all-gather.3.cloned.1.call-done) | copy-start | bytes 16515076
  162.7 2.0 copy-start.6
  164.7 2.7 copy-start.7
  255.0 5.4 %copy-start.4 = (s32[128,4]{0,1:T(4,128)S(1)}, s32[128,4]{0,1:T(4,128)}, u32[]{:S(2)}) copy-start(s32[128,4]{0,1:T(4,128)} %param.10) | copy-start | bytes 6148
  255.0 5.7 %copy-start.5 = (f32[128,4]{0,1:T(4,128)S(1)}, f32[128,4]{0,1:T(4,128)}, u32[]{:S(2)}) copy-start(f32[128,4]{0,1:T(4,128)} %param.11) | copy-start | bytes 6148
  256.6 18.3 %all-to-all-start.3 = ((bf16[4,2,71680]{2,0,1:T(4,128)(2,1)}), bf16[4,2,71680]{2,0,1:T(4,128)(2,1)S(1)}, u32[]{:S(2)}, u32[]{:S(2)}) async-start(bf16[4,2,71680]{2,0,1:T(4,128)(2,1)} %copy.49), calls=%async_computation.3 | async-start | bytes 2293760 | tf_op jit(solution)/shard_map/all_to_all | solution.py:74
  279.4 3.6 %copy-start.1 = (bf16[2048,896]{1,0:T(8,128)(2,1)S(1)}, bf16[2048,896]{1,0:T(8,128)(2,1)}, u32[]{:S(2)}) copy-start(bf16[2048,896]{1,0:T(8,128)(2,1)} %param.17) | copy-start | bytes 11010052
Sparse Core Ops, SparseCore 0:
  54.6 101.8 all-gather.2
  169.1 61.7 all-gather.4
where the time goes:
time: 293 us; the launch traced here: 292 us
  waiting for transfers between devices  178 us (61%)
  blocking collectives  54.7 us (19%)
  matrix products  20.5 us (7%)
  local copies, waits for them, and re-layouts  16.5 us (6%)
  between operations  13.7 us (5%)
  other arithmetic  5.24 us (2%)
  starting transfers between devices  3.82 us (1%)
    all_gather x1, waiting for transfers between devices, local(): segment = lax.all_gather(stacked, 'ctx', axis=1, tiled=True)  102 us
    all_gather x1, waiting for transfers between devices, local(): segment = lax.all_gather(hidden_stack, 'ctx', axis=1, tiled=True)  61.9 us
    all_to_all x1, blocking collectives, local(): lax.all_to_all(send_rows, 'node', split_axis=0, concat_axis=0, tiled=True)  19.6 us
    dot_general x6, matrix products, matmul(): return jnp.dot(left_side, right_side, preferred_element_type=jnp.float32)  18.2 us
    all_to_all x1, blocking collectives, local(): lax.all_to_all(sendback, 'node', split_axis=0, concat_axis=0, tiled=True)  18 us
    all_to_all x1, blocking collectives, local(): lax.all_to_all(lax.all_to_all(send_rows, 'node', split_axis=0, concat_axi...  17.1 us
    all_to_all x1, waiting for transfers between devices, local(): lax.all_to_all(lax.all_to_all(sendback, 'node', split_axis=0, concat_axis...  13.9 us
  transfers between devices with their start and end apart: 3, of which 3 were waited for; matrix products, arithmetic and copies ran while one was open for 0% of the time, Pallas kernels for 0%

commit v1 on v0

--- a/solution.py
+++ b/solution.py
@@ -66,7 +66,7 @@
     routed_hidden = (jax.nn.silu(gate_routed) * up_routed).astype(jnp.bfloat16)
     shared_hidden = (jax.nn.silu(gate_shared) * up_shared).astype(jnp.bfloat16)
     hidden_stack = jnp.concatenate([routed_hidden, shared_hidden], axis=0)
-    segment = lax.all_gather(hidden_stack, "ctx", axis=1, tiled=True)
+    segment = jnp.concatenate(lax.all_gather(hidden_stack, "ctx"), axis=1)
     routed_out = matmul(segment[:slot_total], down_local)
     shared_out = matmul(segment[slot_total:], shared_down)
     routed_bf = routed_out.astype(jnp.bfloat16)

time: 293 us -> 302 us (1.031)
  local copies, waits for them, and re-layouts: 16.5 us -> 27.1 us
    all_gather x0 -> x1, local copies, waits for them, and re-layouts: none -> 3.18 us  [local(): segment = jnp.concatenate(lax.all_gather(hidden_stack, 'ctx'), axis=1)]
    reshape x1, local copies, waits for them, and re-layouts: 0.36 us -> 3.52 us  [local(): routed_bf.reshape(group_count, member_count, capacity * out_width)]
where the time goes in v1:
time: 302 us; the launch traced here: 301 us
  waiting for transfers between devices  177 us (59%)
  blocking collectives  55.7 us (18%)
  local copies, waits for them, and re-layouts  27.1 us (9%)
  matrix products  17.7 us (6%)
  between operations  13.7 us (5%)
  other arithmetic  5.24 us (2%)
  starting transfers between devices  4.67 us (2%)
    all_gather x1, waiting for transfers between devices, local(): segment = lax.all_gather(stacked, 'ctx', axis=1, tiled=True)  102 us
    all_gather x1, waiting for transfers between devices, local(): segment = jnp.concatenate(lax.all_gather(hidden_stack, 'ctx'), axis=1)  61.9 us
    all_to_all x1, blocking collectives, local(): lax.all_to_all(send_rows, 'node', split_axis=0, concat_axis=0, tiled=True)  19.6 us
    all_to_all x1, blocking collectives, local(): lax.all_to_all(sendback, 'node', split_axis=0, concat_axis=0, tiled=True)  19 us
    all_to_all x1, blocking collectives, local(): lax.all_to_all(lax.all_to_all(send_rows, 'node', split_axis=0, concat_axi...  17.1 us
    dot_general x6, matrix products, matmul(): return jnp.dot(left_side, right_side, preferred_element_type=jnp.float32)  15.4 us
    all_to_all x1, waiting for transfers between devices, local(): lax.all_to_all(lax.all_to_all(sendback, 'node', split_axis=0, concat_axis...  13.2 us
  transfers between devices with their start and end apart: 3, of which 3 were waited for; matrix products, arithmetic and copies ran while one was open for 0% of the time, Pallas kernels for 0%

profile of v1, /device:TPU:0, one launch (start us, length us, event | category | flops | bytes accessed | tf_op | source)
XLA Modules:
  0.0 301.1 jit_solution(10338365601813335526)
XLA Ops:
  6.5 0.8 copy.47
  7.3 0.1 eq.52
  7.4 0.1 reshape.115
  7.6 1.1 reduce-window.6
  8.7 0.2 slice_reduce_fusion
  9.0 0.1 fusion.35
  9.1 0.2 fusion.26
  9.3 0.2 select_reduce_fusion
  9.5 1.0 concatenate.9
  10.5 3.1 %gather_fusion = bf16[640,896]{1,0:T(8,128)(2,1)S(1)} fusion(bf16[129,896]{1,0:T(8,128)(2,1)S(1)} %concatenate.9, s32[1024]{0:T(1024)S(1)} %pad_clamp_fusion.1), kind=kCustom, calls=%fused_computation | custom fusion | bytes 2296320 | tf_op jit(solution)/shard_map/gather | solution.py:49
  13.6 0.4 reshape.117
  14.0 19.6 %all_to_all.20 = bf16[4,2,71680]{2,1,0:T(2,128)(2,1)S(1)} all-to-all(bf16[4,2,71680]{2,1,0:T(2,128)(2,1)S(1)} %reshape.117), channel_id=1, replica_groups=mesh['ctx'=4,'node'=4,'local'=2] {'node'}, dimensions={0} | all-to-all | bytes 2293760 | tf_op jit(solution)/shard_map/all_to_all | solution.py:51
  33.5 0.6 copy.49
  34.1 17.1 %all_to_all.21 = bf16[4,2,71680]{2,0,1:T(4,128)(2,1)S(1)} all-to-all(bf16[4,2,71680]{2,0,1:T(4,128)(2,1)S(1)} %copy.49), channel_id=1, replica_groups=mesh['ctx'=4,'node'=4,'local'=2] {'local'}, dimensions={1} | all-to-all | bytes 2293760 | tf_op jit(solution)/shard_map/all_to_all | solution.py:50
  51.3 1.2 copy.50
  52.4 0.8 reshape.118
  53.3 1.2 pad_maximum_fusion
  54.5 0.0 all-gather.4.cloned.1.call-update
  54.5 0.0 all-gather.6.cloned.1.call-start
  54.6 102.0 %all-gather.4.cloned.1.call-done = bf16[768,3584]{1,0:T(8,128)(2,1)} async-done(((bf16[768,896]{1,0:T(8,128)(2,1)}), bf16[768,3584]{1,0:T(8,128)(2,1)}) %all-gather.4.cloned.1.call-update) | async-done | bytes 5505040 | tf_op jit(solution)/shard_map/all_gather | solution.py:59
  156.6 6.1 %fusion.2 = f32[640,512]{1,0:T(8,128)S(1)} fusion(bf16[768,3584]{1,0:T(8,128)(2,1)} %all-gather.4.cloned.1.call-done, bf16[1,3584,512]{2,1,0:T(8,128)(2,1)} %param.12), kind=kOutput, calls=%fused_computation.4 | convolution fusion | flops 2348810240 | bytes 9568256 | tf_op jit(solution)/shard_map/dot_general | solution.py:10
  162.7 0.6 fusion.31
  163.3 1.4 copy-done.7
  164.7 2.6 fusion.21
  167.4 0.6 fusion.28
  168.0 0.9 pad_maximum_fusion.1
  169.0 61.9 %all-gather.6.cloned.1.call-done = bf16[3072,512]{1,0:T(8,128)(2,1)} async-done(((bf16[768,512]{1,0:T(8,128)(2,1)}), bf16[3072,512]{1,0:T(8,128)(2,1)}) %all-gather.6.cloned.1.call-update) | async-done | bytes 3145744 | tf_op jit(solution)/shard_map/all_gather | solution.py:69
  230.9 3.2 %copy.51 = bf16[4,768,512]{1,2,0:T(8,128)(2,1)S(1)} copy(bf16[4,768,512]{2,1,0:T(8,128)(2,1)} %bitcast.36) | data formatting | bytes 6291456 | tf_op jit(solution)/shard_map/all_gather | solution.py:69
  234.1 0.2 slice.40
  234.3 1.8 copy-done.9
  236.1 4.0 %fusion.10 = bf16[640,896]{1,0:T(8,128)(2,1)} fusion(bf16[640,2048]{0,1:T(8,128)(2,1)S(1)} %bitcast.37, bf16[1,2048,896]{2,1,0:T(8,128)(2,1)S(1)} %copy-done.9), kind=kOutput, calls=%fused_computation.13 | convolution fusion | flops 2349383680 | bytes 7438336 | tf_op jit(solution)/shard_map/dot_general | solution.py:10
  240.1 3.5 %reshape.120 = bf16[4,2,71680]{2,1,0:T(2,128)(2,1)} reshape(bf16[640,896]{1,0:T(8,128)(2,1)} %fusion.10) | data formatting | bytes 2293760 | tf_op jit(solution)/shard_map/reshape | solution.py:73
  243.6 19.0 %all_to_all.22 = bf16[4,2,71680]{2,1,0:T(2,128)(2,1)S(1)} all-to-all(bf16[4,2,71680]{2,1,0:T(2,128)(2,1)} %reshape.120), channel_id=1, replica_groups=mesh['ctx'=4,'node'=4,'local'=2] {'node'}, dimensions={0} | all-to-all | bytes 2293760 | tf_op jit(solution)/shard_map/all_to_all | solution.py:75
  262.6 1.6 copy.54
  264.2 4.6 %all-to-all-start.3 = ((bf16[4,2,71680]{2,0,1:T(4,128)(2,1)}), bf16[4,2,71680]{2,0,1:T(4,128)(2,1)}, u32[]{:S(2)}, u32[]{:S(2)}) async-start(bf16[4,2,71680]{2,0,1:T(4,128)(2,1)} %copy.54), calls=%async_computation.3 | async-start | bytes 2293760 | tf_op jit(solution)/shard_map/all_to_all | solution.py:74
  268.9 0.1 copy.56
  269.0 0.1 mul.67
  269.1 0.1 copy.52
  269.2 0.1 copy.53
  269.4 0.9 slice.39
  270.3 13.2 %all-to-all-done.3 = bf16[4,2,71680]{2,0,1:T(4,128)(2,1)} async-done(((bf16[4,2,71680]{2,0,1:T(4,128)(2,1)}), bf16[4,2,71680]{2,0,1:T(4,128)(2,1)}, u32[]{:S(2)}, u32[]{:S(2)}) %all-to-all-start.3) | async-done | bytes 1146912 | tf_op jit(solution)/shard_map/all_to_all | solution.py:74
  283.4 2.4 copy.55
  285.9 0.8 reshape.121
  286.7 2.1 gather_fusion.1
  288.7 0.5 reshape.122
  289.2 2.3 fusion.13
  291.6 1.3 convert_reduce_fusion
  292.9 1.4 fusion.27
  (32 shorter events, 0.2 us)
Async XLA Ops:
  6.5 150.0 %all-gather.4.cloned.1.call-start = ((), (), s32[]{:S(2)}) async-start(), calls=%async_computation.4 | async-start | bytes 6881280 | tf_op jit(solution)/shard_map/all_gather | solution.py:59
  51.3 2.0 copy-start.3
  54.5 176.4 %all-gather.6.cloned.1.call-start = ((), (), s32[]{:S(2)}) async-start(), calls=%async_computation.5 | async-start | bytes 3932160 | tf_op jit(solution)/shard_map/all_gather | solution.py:69
  156.6 6.1 %copy-start = (bf16[3584,512]{1,0:T(8,128)(2,1)S(1)}, bf16[3584,512]{1,0:T(8,128)(2,1)}, u32[]{:S(2)}) copy-start(bf16[3584,512]{1,0:T(8,128)(2,1)} %param.15) | copy-start | bytes 11010052
  156.6 6.1 %copy-start.4 = (bf16[768,3584]{1,0:T(8,128)(2,1)S(1)}, bf16[768,3584]{1,0:T(8,128)(2,1)}, u32[]{:S(2)}) copy-start(bf16[768,3584]{1,0:T(8,128)(2,1)} %all-gather.4.cloned.1.call-done) | copy-start | bytes 16515076
  162.7 2.0 copy-start.7
  164.7 2.7 copy-start.8
  234.1 2.0 copy-start.9
  262.6 6.3 %copy-start.5 = (s32[128,4]{0,1:T(4,128)S(1)}, s32[128,4]{0,1:T(4,128)}, u32[]{:S(2)}) copy-start(s32[128,4]{0,1:T(4,128)} %param.10) | copy-start | bytes 6148
  262.6 6.6 %copy-start.6 = (f32[128,4]{0,1:T(4,128)S(1)}, f32[128,4]{0,1:T(4,128)}, u32[]{:S(2)}) copy-start(f32[128,4]{0,1:T(4,128)} %param.11) | copy-start | bytes 6148
  264.2 19.2 %all-to-all-start.3 = ((bf16[4,2,71680]{2,0,1:T(4,128)(2,1)}), bf16[4,2,71680]{2,0,1:T(4,128)(2,1)}, u32[]{:S(2)}, u32[]{:S(2)}) async-start(bf16[4,2,71680]{2,0,1:T(4,128)(2,1)} %copy.54), calls=%async_computation.3 | async-start | bytes 2293760 | tf_op jit(solution)/shard_map/all_to_all | solution.py:74
  289.2 3.6 %copy-start.1 = (bf16[2048,896]{1,0:T(8,128)(2,1)S(1)}, bf16[2048,896]{1,0:T(8,128)(2,1)}, u32[]{:S(2)}) copy-start(bf16[2048,896]{1,0:T(8,128)(2,1)} %param.17) | copy-start | bytes 11010052
  289.2 3.6 %copy-start.2 = (bf16[128,4,512]{0,2,1:T(8,128)(2,1)S(1)}, bf16[128,4,512]{0,2,1:T(8,128)(2,1)}, u32[]{:S(2)}) copy-start(bf16[128,4,512]{0,2,1:T(8,128)(2,1)} %slice.39) | copy-start | bytes 1572868
Sparse Core Ops, SparseCore 0:
  54.6 101.8 all-gather.3
  169.1 61.7 all-gather.5
